TPU v7x, 32 devices: a whole 2x2x4 slice. The times are simulated.
32 devices in a mesh: seq: 4 (over z), head: 2 (over y), dp: 4 (over x, core).
Axes of the slice: x: 2, y: 2, z: 4, core: 2. Of those that a mesh axis runs over, the one named last changes fastest.
Arguments:
- layer_input: bfloat16 [4, 512, 6144], P('dp', 'seq'), may hold values from -6 to 6
- queries: bfloat16 [4, 512, 1024], P('dp', 'seq', 'head'), may hold values from -6 to 6
- key_rows: bfloat16 [4, 512, 1024], P('dp', 'seq', 'head'), may hold values from -6 to 6
- value_rows: bfloat16 [4, 512, 1024], P('dp', 'seq', 'head'), may hold values from -6 to 6
- grad_out: bfloat16 [4, 512, 1024], P('dp', 'seq', 'head'), may hold values from -6 to 6
- log_decay: float32 [4, 512, 8], P('dp', 'seq', 'head'), may hold values from -2 to 0, as said below
Outputs:
- grad_query: bfloat16 [4, 512, 1024], P('dp', 'seq', 'head')
- grad_key: bfloat16 [4, 512, 1024], P('dp', 'seq', 'head')
- grad_value: bfloat16 [4, 512, 1024], P('dp', 'seq', 'head')
- key_weight_grad: bfloat16 [6144, 1024], P('seq', 'head')
- value_weight_grad: bfloat16 [6144, 1024], P('seq', 'head')
Inputs may be any that keep to these rules, and one draw needn't show every extreme that they name: log_decay is never positive.
All inputs are finite; a program needn't handle non-finite values.
Results may differ from a plain program's by a relative error of at most 0.0062.
Values may be sent and summed in bfloat16 or wider, within the bound.
A program may use at most 64 MiB of HBM per device.

v0:
```python
import math
import jax
import jax.numpy as jnp
from jax import lax
from jax.sharding import PartitionSpec as P

DH = 128
top_precision = lax.Precision.HIGHEST


def per_device(layer_input, queries, key_rows, value_rows, grad_out, log_decay):
    length = queries.shape[1]
    heads = log_decay.shape[2]
    query_three = queries[0].reshape(length, heads, DH)
    key_three = key_rows[0].reshape(length, heads, DH)
    triple_value = value_rows[0].reshape(length, heads, DH)
    triple_gradient = grad_out[0].reshape(length, heads, DH)
    running = jnp.cumsum(log_decay[0], axis=0)
    totals = running[-1]
    across = running.T
    positions = jnp.arange(length)
    lower_mask = positions[:, None] >= positions[None, :]
    decay_mask = jnp.where(
        lower_mask[None], jnp.exp(jnp.minimum(across[:, :, None] - across[:, None, :], 0.0)), 0.0
    )
    to_end = jnp.exp(totals[None, :] - running)
    from_start = jnp.exp(running)
    key_rows_scaled = (key_three * to_end[:, :, None]).astype(jnp.bfloat16)
    scaled_queries = (query_three * from_start[:, :, None]).astype(jnp.bfloat16)
    key_state = jnp.einsum(
        "nrx,nro->rxo", key_rows_scaled, triple_value, preferred_element_type=jnp.float32
    )
    query_state = jnp.einsum(
        "thq,thv->hqv", scaled_queries, triple_gradient, preferred_element_type=jnp.float32
    )
    every_key_row, all_queries, all_totals = (
        lax.all_gather(key_state[None], "seq", axis=0, tiled=True),
        lax.all_gather(query_state[None], "seq", axis=0, tiled=True),
        lax.all_gather(totals[None], "seq", axis=0, tiled=True),
    )
    count = lax.axis_size("seq")
    here = lax.axis_index("seq")
    through = jnp.cumsum(all_totals, axis=0)
    before = through - all_totals
    block_ids = jnp.arange(count)[:, None]
    own_before = lax.dynamic_index_in_dim(before, here, 0, keepdims=False)
    own_through = lax.dynamic_index_in_dim(through, here, 0, keepdims=False)
    leading_weight = jnp.where(
        block_ids < here, jnp.exp(jnp.minimum(own_before[None] - through, 0.0)), 0.0
    )
    late_weight = jnp.where(
        block_ids > here, jnp.exp(jnp.minimum(before - own_through[None], 0.0)), 0.0
    )
    prefix_running = jnp.einsum(
        "cp,cpqt->pqt", leading_weight, every_key_row, precision=top_precision
    )
    suffix = jnp.einsum("nh,nhqv->hqv", late_weight, all_queries, precision=top_precision)
    prefix_reduced = prefix_running.astype(jnp.bfloat16)
    suffix_low = suffix.astype(jnp.bfloat16)
    value_scores = jnp.einsum(
        "thv,jhv->htj", triple_gradient, triple_value, preferred_element_type=jnp.float32
    )
    value_weights = (value_scores * decay_mask).astype(jnp.bfloat16)
    key_scores = jnp.einsum(
        "thq,jhq->htj", query_three, key_three, preferred_element_type=jnp.float32
    )
    key_weights = (key_scores * decay_mask).astype(jnp.bfloat16)
    scale = 1.0 / DH
    query_grad = (
        jnp.einsum("htj,jhk->thk", value_weights, key_three, preferred_element_type=jnp.float32)
        + from_start[:, :, None]
        * jnp.einsum(
            "jfg,xjg->xjf", prefix_reduced, triple_gradient, preferred_element_type=jnp.float32
        )
    ) * scale
    key_grad = (
        jnp.einsum("htj,thq->jhq", value_weights, query_three, preferred_element_type=jnp.float32)
        + to_end[:, :, None]
        * jnp.einsum("hqv,jhv->jhq", suffix_low, triple_value, preferred_element_type=jnp.float32)
    ) * scale
    value_grad = (
        jnp.einsum("htj,thv->jhv", key_weights, triple_gradient, preferred_element_type=jnp.float32)
        + to_end[:, :, None]
        * jnp.einsum("hqv,jhq->jhv", suffix_low, key_three, preferred_element_type=jnp.float32)
    ) * scale
    grad_query = query_grad.astype(jnp.bfloat16).reshape(1, length, heads * DH)
    grad_key = key_grad.astype(jnp.bfloat16).reshape(1, length, heads * DH)
    grad_value = value_grad.astype(jnp.bfloat16).reshape(1, length, heads * DH)
    columns = lax.all_to_all(layer_input, "seq", split_axis=2, concat_axis=1, tiled=True)
    rows = columns[0]
    dims = (((0,), (0,)), ((), ()))
    key_part = lax.dot_general(
        rows,
        lax.all_gather(grad_key, "seq", axis=1, tiled=True)[0],
        dims,
        preferred_element_type=jnp.float32,
    )
    value_part = lax.dot_general(
        rows,
        lax.all_gather(grad_value, "seq", axis=1, tiled=True)[0],
        dims,
        preferred_element_type=jnp.float32,
    )
    factor = 1.0 / math.sqrt(lax.axis_size("dp") * lax.axis_size("seq") * layer_input.shape[1])
    key_summed, value_summed = lax.psum((key_part, value_part), "dp")
    key_weight_grad = (key_summed * factor).astype(jnp.bfloat16)
    value_weight_grad = (value_summed * factor).astype(jnp.bfloat16)
    return (grad_query, grad_key, grad_value, key_weight_grad, value_weight_grad)


def solution(mesh):
    return jax.shard_map(
        per_device,
        mesh=mesh,
        in_specs=(
            P("dp", "seq", None),
            P("dp", "seq", "head"),
            P("dp", "seq", "head"),
            P("dp", "seq", "head"),
            P("dp", "seq", "head"),
            P("dp", "seq", "head"),
        ),
        out_specs=(
            P("dp", "seq", "head"),
            P("dp", "seq", "head"),
            P("dp", "seq", "head"),
            P("seq", "head"),
            P("seq", "head"),
        ),
        check_vma=False,
    )
```

profile of v0, /device:TPU:0, one launch (start us, length us, event | category | flops | bytes accessed | tf_op | source)
XLA Modules:
  0.0 296.4 jit_solution(7479897676144758266)
XLA Ops:
  7.2 0.0 all-gather.8.cloned.1.call-start
  7.2 0.8 copy.80
  8.0 0.2 reduce_window_sum.22
  8.2 0.1 copy.84
  8.3 1.0 copy.88
  9.3 1.0 copy.119
  10.4 0.9 fusion.19
  11.3 6.8 %copy.96 = bf16[1,128,6144]{1,0,2:T(2,128)(2,1)S(1)} copy(bf16[1,128,6144]{2,1,0:T(8,128)(2,1)} %param.6) | data formatting | bytes 3145728 | tf_op args[0]
  18.2 0.5 broadcast.43
  18.7 34.4 %reduce.2 = bf16[6144,128]{1,0:T(8,128)(2,1)} reduce(bf16[6144,1,128]{2,1,0:T(2,128)(2,1)S(1)} %bitcast.97, bf16[]{:T(256)} %broadcast.43), dimensions={1}, to_apply=%bitcast.77.reduce_sub_computation | reduce | bytes 3145730
  53.1 3.7 %reshape.75 = bf16[4,2,98304]{2,1,0:T(2,128)(2,1)} reshape(bf16[6144,128]{1,0:T(8,128)(2,1)} %reduce.2) | data formatting | bytes 3145728
  56.8 6.5 %all-to-all-start = ((bf16[4,2,98304]{2,1,0:T(2,128)(2,1)}), bf16[4,2,98304]{2,1,0:T(2,128)(2,1)}, u32[]{:S(2)}, u32[]{:S(2)}) async-start(bf16[4,2,98304]{2,1,0:T(2,128)(2,1)} %reshape.75), calls=%async_computation | async-start | bytes 3145728 | tf_op jit(solution)/shard_map/all_to_all | solution.py:89
  63.3 0.1 copy.85
  63.3 0.1 reshape_squeeze.13
  63.4 0.1 copy.83
  63.5 0.9 fusion.18
  64.4 0.0 all-reduce.3.cloned.1.call-start
  64.5 44.7 %all-gather.2 = f32[4,1,4]{2,1,0:T(1,128)S(1)} all-gather(f32[1,1,4]{2,1,0:T(1,128)S(1)} %get-tuple-element.32), channel_id=1, replica_groups=mesh['seq'=4,'head'=2,'dp'=4] {'seq'}, dimensions={0}, use_global_device_ids=true | all-gather | bytes 80 | tf_op jit(solution)/shard_map/all_gather | solution.py:39
  109.1 0.1 copy.81
  109.3 0.1 select_bitcast_fusion
  109.4 0.2 fusion.12
  109.7 1.4 multiply_reduce_fusion
  111.1 0.1 copy.112
  111.2 0.2 fusion.5
  111.5 0.2 fusion.10
  111.6 23.9 %all_gather.18 = bf16[1,512,512]{1,2,0:T(8,128)(2,1)} all-gather(bf16[1,128,512]{1,2,0:T(8,128)(2,1)S(1)} %bitcast.104), channel_id=1, replica_groups=mesh['seq'=4,'head'=2,'dp'=4] {'seq'}, dimensions={1}, use_global_device_ids=true | all-gather | bytes 655360 | tf_op jit(solution)/shard_map/all_gather | solution.py:94
  135.5 0.2 fusion.4
  135.7 0.4 fusion.11
  136.1 14.7 %all_gather.19 = bf16[1,512,512]{1,2,0:T(8,128)(2,1)} all-gather(bf16[1,128,512]{1,2,0:T(8,128)(2,1)S(1)} %bitcast.117), channel_id=1, replica_groups=mesh['seq'=4,'head'=2,'dp'=4] {'seq'}, dimensions={1}, use_global_device_ids=true | all-gather | bytes 655360 | tf_op jit(solution)/shard_map/all_gather | solution.py:100
  150.8 3.1 %reshape.76 = bf16[6144,1,128]{2,1,0:T(2,128)(2,1)S(1)} reshape(bf16[4,2,98304]{2,1,0:T(2,128)(2,1)} %all-to-all-done) | data formatting | bytes 3145728
  153.8 1.3 copy.117
  155.2 1.8 copy.97
  157.0 2.6 convolution_bitcast_fusion
  159.6 2.6 convolution_bitcast_fusion.1
  162.3 0.1 select_bitcast_fusion.1
  162.4 0.1 copy.103
  162.5 0.7 copy-done.10
  163.2 0.2 convolution_bitcast_fusion.7
  163.4 0.8 copy.100
  164.1 0.8 copy.99
  164.9 3.6 %fusion.14 = f32[4,1,128,128]{3,1,2,0:T(1,128)S(1)} fusion(f32[4,4,1,1]{0,2,3,1:T(1,128)S(1)} %copy.103, f32[4,4,128,128]{3,2,1,0:T(8,128)} %bitcast.114), kind=kOutput, calls=%fused_computation.27 | convolution fusion | flops 3145728 | bytes 1310784 | tf_op jit(solution)/shard_map/cp,cpqt->pqt/dot_general | solution.py:54
  168.5 0.2 fusion.9
  168.7 0.8 copy.98
  169.5 112.8 %all-reduce.3.cloned.1.call-done = (f32[1536,512]{0,1:T(8,128)}, f32[1536,512]{0,1:T(8,128)}) async-done(((f32[1536,512]{0,1:T(8,128)}, f32[1536,512]{0,1:T(8,128)}), (f32[1536,512]{0,1:T(8,128)}, f32[1536,512]{0,1:T(8,128)})) %all-reduce.3.cloned.1.call-update) | async-done | bytes 6291472 | tf_op jit(solution)/shard_map/psum | solution.py:105
  282.2 2.2 multiply_convert_fusion.1
  284.5 1.6 copy.101
  286.0 2.2 multiply_convert_fusion
  288.3 1.6 copy.102
  (39 shorter events, 0.3 us)
Async XLA Ops:
  7.2 102.5 %all-gather.8.cloned.1.call-start = ((), (), s32[]{:S(2)}) async-start(), calls=%async_computation.2 | async-start | bytes 1310720 | tf_op jit(solution)/shard_map/all_gather | solution.py:38
  8.2 10.0 %copy-start.5 = (f32[128,4]{1,0:T(8,128)}, f32[128,4]{1,0:T(8,128)S(1)}, u32[]{:S(2)}) copy-start(f32[128,4]{1,0:T(8,128)S(1)} %reduce_window_sum.22) | copy-start | bytes 6148
  10.4 99.0 %copy-start.2 = (bf16[1,128,512]{1,2,0:T(8,128)(2,1)}, bf16[1,128,512]{1,2,0:T(8,128)(2,1)S(1)}, u32[]{:S(2)}) copy-start(bf16[1,128,512]{1,2,0:T(8,128)(2,1)S(1)} %copy.119) | copy-start | bytes 393220
  56.8 6.5 %copy-start.11 = (bf16[1,128,512]{2,1,0:T(8,128)(2,1)S(1)}, bf16[1,128,512]{2,1,0:T(8,128)(2,1)}, u32[]{:S(2)}) copy-start(bf16[1,128,512]{2,1,0:T(8,128)(2,1)} %param.9) | copy-start | bytes 393220
  56.8 6.6 %copy-start.12 = (bf16[1,128,512]{2,1,0:T(8,128)(2,1)S(1)}, bf16[1,128,512]{2,1,0:T(8,128)(2,1)}, u32[]{:S(2)}) copy-start(bf16[1,128,512]{2,1,0:T(8,128)(2,1)} %param.8) | copy-start | bytes 393220
  56.8 52.3 %copy-start.6 = (f32[128,4]{1,0:T(8,128)S(1)}, f32[128,4]{1,0:T(8,128)}, u32[]{:S(2)}) copy-start(f32[128,4]{1,0:T(8,128)} %copy-done.5) | copy-start | bytes 6148
  56.8 94.0 %all-to-all-start = ((bf16[4,2,98304]{2,1,0:T(2,128)(2,1)}), bf16[4,2,98304]{2,1,0:T(2,128)(2,1)}, u32[]{:S(2)}, u32[]{:S(2)}) async-start(bf16[4,2,98304]{2,1,0:T(2,128)(2,1)} %reshape.75), calls=%async_computation | async-start | bytes 3145728 | tf_op jit(solution)/shard_map/all_to_all | solution.py:89
  63.3 101.6 %all-gather.6.cloned.1.call-start = ((), (), s32[]{:S(2)}) async-start(), calls=%async_computation.1 | async-start | bytes 1310720 | tf_op jit(solution)/shard_map/all_gather | solution.py:37
  64.4 217.8 %all-reduce.3.cloned.1.call-start = ((), (), s32[]{:S(2)}) async-start(), calls=%async_computation.3 | async-start | bytes 12582912 | tf_op jit(solution)/shard_map/psum | solution.py:105
  109.6 25.9 %copy-start.9 = (bf16[4,128,128]{2,1,0:T(8,128)(2,1)}, bf16[4,128,128]{2,1,0:T(8,128)(2,1)S(1)}, u32[]{:S(2)}) copy-start(bf16[4,128,128]{2,1,0:T(8,128)(2,1)S(1)} %fusion.12) | copy-start | bytes 393220
  111.1 24.7 %copy-start.3 = (bf16[1,128,512]{1,2,0:T(8,128)(2,1)S(1)}, bf16[1,128,512]{1,2,0:T(8,128)(2,1)}, u32[]{:S(2)}) copy-start(bf16[1,128,512]{1,2,0:T(8,128)(2,1)} %copy-done.2) | copy-start | bytes 393220
  136.1 14.7 %copy-start.7 = (bf16[128,4,128]{0,2,1:T(8,128)(2,1)}, bf16[128,4,128]{0,2,1:T(8,128)(2,1)S(1)}, u32[]{:S(2)}) copy-start(bf16[128,4,128]{0,2,1:T(8,128)(2,1)S(1)} %fusion.11) | copy-start | bytes 393220
  155.2 1.8 copy-start.1
  157.0 2.6 copy-start
  162.3 0.9 copy-start.10
  162.3 1.1 copy-start.8
  162.3 6.2 %copy-start.4 = (bf16[1,128,512]{1,2,0:T(8,128)(2,1)S(1)}, bf16[1,128,512]{1,2,0:T(8,128)(2,1)}, u32[]{:S(2)}) copy-start(bf16[1,128,512]{1,2,0:T(8,128)(2,1)} %copy-done.2) | copy-start | bytes 393220
Sparse Core Ops, SparseCore 0:
  11.4 30.6 all-gather.7
  65.7 45.5 all-gather.5
  162.4 119.7 all-reduce.2
where the time goes:
time: 297 us; the launch traced here: 296 us
  waiting for transfers between devices  113 us (38%)
  blocking collectives  83.2 us (28%)
  other arithmetic  40.7 us (14%)
  local copies, waits for them, and re-layouts  26.9 us (9%)
  between operations  14 us (5%)
  matrix products  12.2 us (4%)
  starting transfers between devices  6.54 us (2%)
    psum x1, waiting for transfers between devices, per_device(): key_summed, value_summed = lax.psum((key_part, value_part), 'dp')  113 us
    all_gather x1, blocking collectives, per_device(): lax.all_gather(totals[None], 'seq', axis=0, tiled=True)  44.7 us
    unnamed x3, other arithmetic  35.9 us
    all_gather x1, blocking collectives, per_device(): lax.all_gather(grad_key, 'seq', axis=1, tiled=True)[0]  23.9 us
    unnamed x38, local copies, waits for them, and re-layouts  22.8 us
    all_gather x1, blocking collectives, per_device(): lax.all_gather(grad_value, 'seq', axis=1, tiled=True)[0]  14.7 us
    all_to_all x1, starting transfers between devices, per_device(): lax.all_to_all(layer_input, 'seq', split_axis=2, concat_axis=1, tiled=True)  6.46 us
  transfers between devices with their start and end apart: 4, of which 1 were waited for; matrix products, arithmetic and copies ran while one was open for 23% of the time, Pallas kernels for 0%

commit v1 on v0

--- a/solution.py
+++ b/solution.py
@@ -86,7 +86,12 @@
     grad_query = query_grad.astype(jnp.bfloat16).reshape(1, length, heads * DH)
     grad_key = key_grad.astype(jnp.bfloat16).reshape(1, length, heads * DH)
     grad_value = value_grad.astype(jnp.bfloat16).reshape(1, length, heads * DH)
-    columns = lax.all_to_all(layer_input, "seq", split_axis=2, concat_axis=1, tiled=True)
+    columns = jnp.concatenate(
+        lax.all_to_all(
+            jnp.stack(jnp.split(layer_input, lax.axis_size("seq"), axis=2)), "seq", 0, 0
+        ),
+        axis=1,
+    )
     rows = columns[0]
     dims = (((0,), (0,)), ((), ()))
     key_part = lax.dot_general(

time: 297 us -> 255 us (0.86)
  other arithmetic: 40.7 us -> 8.33 us
  local copies, waits for them, and re-layouts: 26.9 us -> 6.01 us
  blocking collectives: 83.2 us -> 95.3 us
    unnamed x3 -> x2, other arithmetic: 35.9 us -> 1.43 us
    unnamed x38 -> x13, local copies, waits for them, and re-layouts: 22.8 us -> 3.49 us
    all_gather x1, blocking collectives: 23.9 us -> 32.7 us  [per_device(): lax.all_gather(grad_key, 'seq', axis=1, tiled=True)[0]]
  transfers between devices with their start and end apart: 4 -> 4, of which waited for: 1 -> 1; matrix products, arithmetic and copies ran while one was open for 23% -> 7% of each run, Pallas kernels for 0% -> 0%
where the time goes in v1:
time: 255 us
  waiting for transfers between devices  113 us (44%)
  blocking collectives  95.3 us (37%)
  between operations  13.9 us (5%)
  matrix products  12.4 us (5%)
  other arithmetic  8.33 us (3%)
  starting transfers between devices  6.53 us (3%)
  local copies, waits for them, and re-layouts  6.01 us (2%)
    psum x1, waiting for transfers between devices, per_device(): key_summed, value_summed = lax.psum((key_part, value_part), 'dp')  113 us
    all_gather x1, blocking collectives, per_device(): lax.all_gather(totals[None], 'seq', axis=0, tiled=True)  46.9 us
    all_gather x1, blocking collectives, per_device(): lax.all_gather(grad_key, 'seq', axis=1, tiled=True)[0]  32.7 us
    all_gather x1, blocking collectives, per_device(): lax.all_gather(grad_value, 'seq', axis=1, tiled=True)[0]  15.7 us
    all_to_all x1, starting transfers between devices, per_device(): lax.all_to_all(jnp.stack(jnp.split(layer_input, lax.axis_size('seq'), axi...  6.45 us
  transfers between devices with their start and end apart: 4, of which 1 were waited for; matrix products, arithmetic and copies ran while one was open for 7% of the time, Pallas kernels for 0%

profile of v1, /device:TPU:0, one launch (start us, length us, event | category | flops | bytes accessed | tf_op | source)
XLA Modules:
  0.0 255.1 jit_solution(13802505923629396627)
XLA Ops:
  7.2 0.0 copy-start.1
  7.2 0.0 all-gather.8.cloned.1.call-start
  7.2 0.9 copy.32
  8.1 0.2 reduce_window_sum.22
  8.3 0.1 copy.36
  8.4 1.0 copy.40
  9.4 1.0 copy.62
  10.5 0.9 fusion.21
  11.4 0.0 all-gather.8.cloned.1.call-update
  11.4 0.0 copy-done.1
  11.4 0.1 slice_bitcast_fusion.3
  11.6 1.3 pad_maximum_fusion
  12.9 6.4 %all-to-all-start = ((bf16[4,1,128,1536]{3,2,1,0:T(8,128)(2,1)}), bf16[4,1,128,1536]{3,2,1,0:T(8,128)(2,1)S(1)}, u32[]{:S(2)}, u32[]{:S(2)}) async-start(bf16[4,1,128,1536]{3,2,1,0:T(8,128)(2,1)} %pad_maximum_fusion), calls=%async_computation | async-start | bytes 3145728 | tf_op jit(solution)/shard_map/all_to_all | solution.py:90
  19.3 0.0 all-gather.6.cloned.1.call-start
  19.3 0.1 copy.37
  19.4 0.1 reshape_squeeze.13
  19.5 0.1 copy.35
  19.6 0.9 fusion.20
  20.5 0.0 all-gather.6.cloned.1.call-update
  20.5 0.0 all-reduce.3.cloned.1.call-start
  20.6 46.9 %all-gather.2 = f32[4,1,4]{2,1,0:T(1,128)S(1)} all-gather(f32[1,1,4]{2,1,0:T(1,128)S(1)} %get-tuple-element.26), channel_id=1, replica_groups=mesh['seq'=4,'head'=2,'dp'=4] {'seq'}, dimensions={0}, use_global_device_ids=true | all-gather | bytes 80 | tf_op jit(solution)/shard_map/all_gather | solution.py:39
  67.4 0.1 copy.33
  67.6 0.1 select_bitcast_fusion
  67.6 0.2 fusion.12
  67.9 0.0 all-gather.8.cloned.1.call-done
  67.9 1.4 multiply_reduce_fusion
  69.3 0.1 copy.58
  69.4 0.2 fusion.5
  69.7 0.2 fusion.10
  69.9 32.7 %all_gather.18 = bf16[1,512,512]{1,2,0:T(8,128)(2,1)S(1)} all-gather(bf16[1,128,512]{1,2,0:T(8,128)(2,1)S(1)} %bitcast.100), channel_id=1, replica_groups=mesh['seq'=4,'head'=2,'dp'=4] {'seq'}, dimensions={1}, use_global_device_ids=true | all-gather | bytes 655360 | tf_op jit(solution)/shard_map/all_gather | solution.py:99
  102.6 0.2 fusion.4
  102.8 0.4 fusion.11
  103.2 15.7 %all_gather.19 = bf16[1,512,512]{1,2,0:T(8,128)(2,1)S(1)} all-gather(bf16[1,128,512]{1,2,0:T(8,128)(2,1)S(1)} %bitcast.113), channel_id=1, replica_groups=mesh['seq'=4,'head'=2,'dp'=4] {'seq'}, dimensions={1}, use_global_device_ids=true | all-gather | bytes 655360 | tf_op jit(solution)/shard_map/all_gather | solution.py:105
  118.9 0.0 all-to-all-done
  118.9 2.7 %fusion.16 = f32[1536,512]{1,0:T(8,128)} fusion(bf16[512,1536]{1,0:T(8,128)(2,1)S(1)} %bitcast.94, bf16[1,512,512]{1,2,0:T(8,128)(2,1)S(1)} %all_gather.19), kind=kOutput, calls=%fused_computation.28 | convolution fusion | flops 805306368 | bytes 5242880 | tf_op jit(solution)/shard_map/dot_general | solution.py:103
  121.6 2.8 %fusion.18 = f32[1536,512]{1,0:T(8,128)} fusion(bf16[512,1536]{1,0:T(8,128)(2,1)S(1)} %bitcast.95, bf16[1,512,512]{1,2,0:T(8,128)(2,1)S(1)} %all_gather.18), kind=kOutput, calls=%fused_computation.30 | convolution fusion | flops 805306368 | bytes 5242880 | tf_op jit(solution)/shard_map/dot_general | solution.py:97
  124.3 0.0 all-reduce.3.cloned.1.call-update
  124.4 0.1 select_bitcast_fusion.1
  124.4 0.1 copy.49
  124.5 0.2 convolution_bitcast_fusion.5
  124.7 0.8 copy.48
  125.5 0.8 copy.47
  126.3 3.6 %fusion.14 = f32[4,1,128,128]{3,1,2,0:T(1,128)S(1)} fusion(f32[4,4,1,1]{0,2,3,1:T(1,128)S(1)} %copy.49, f32[4,4,128,128]{3,2,1,0:T(8,128)} %bitcast.110), kind=kOutput, calls=%fused_computation.26 | convolution fusion | flops 3145728 | bytes 1310784 | tf_op jit(solution)/shard_map/cp,cpqt->pqt/dot_general | solution.py:54
  129.9 0.2 fusion.9
  130.0 0.8 copy.46
  130.8 112.5 %all-reduce.3.cloned.1.call-done = (f32[1536,512]{1,0:T(8,128)}, f32[1536,512]{1,0:T(8,128)}) async-done(((f32[1536,512]{1,0:T(8,128)}, f32[1536,512]{1,0:T(8,128)}), (f32[1536,512]{1,0:T(8,128)}, f32[1536,512]{1,0:T(8,128)})) %all-reduce.3.cloned.1.call-update) | async-done | bytes 6291472 | tf_op jit(solution)/shard_map/psum | solution.py:110
  243.4 3.6 %multiply_convert_fusion.1 = bf16[1536,512]{1,0:T(8,128)(2,1)} fusion(f32[1536,512]{1,0:T(8,128)} %get-tuple-element.15), kind=kLoop, calls=%fused_computation.1 | loop fusion | flops 1572864 | bytes 4718592 | tf_op jit(solution)/shard_map/convert_element_type | solution.py:111
  247.0 1.6 multiply_convert_fusion
  (14 shorter events, 0.1 us)
Async XLA Ops:
  7.2 4.2 %copy-start.1 = (bf16[1,128,6144]{2,1,0:T(8,128)(2,1)S(1)}, bf16[1,128,6144]{2,1,0:T(8,128)(2,1)}, u32[]{:S(2)}) copy-start(bf16[1,128,6144]{2,1,0:T(8,128)(2,1)} %param.6) | copy-start | bytes 4718596
  7.2 60.7 %all-gather.8.cloned.1.call-start = ((), (), s32[]{:S(2)}) async-start(), calls=%async_computation.2 | async-start | bytes 1310720 | tf_op jit(solution)/shard_map/all_gather | solution.py:38
  12.9 6.5 %copy-start.2 = (bf16[1,128,512]{2,1,0:T(8,128)(2,1)S(1)}, bf16[1,128,512]{2,1,0:T(8,128)(2,1)}, u32[]{:S(2)}) copy-start(bf16[1,128,512]{2,1,0:T(8,128)(2,1)} %param.9) | copy-start | bytes 393220
  12.9 6.6 %copy-start.3 = (bf16[1,128,512]{2,1,0:T(8,128)(2,1)S(1)}, bf16[1,128,512]{2,1,0:T(8,128)(2,1)}, u32[]{:S(2)}) copy-start(bf16[1,128,512]{2,1,0:T(8,128)(2,1)} %param.8) | copy-start | bytes 393220
  12.9 106.0 %all-to-all-start = ((bf16[4,1,128,1536]{3,2,1,0:T(8,128)(2,1)}), bf16[4,1,128,1536]{3,2,1,0:T(8,128)(2,1)S(1)}, u32[]{:S(2)}, u32[]{:S(2)}) async-start(bf16[4,1,128,1536]{3,2,1,0:T(8,128)(2,1)} %pad_maximum_fusion), calls=%async_computation | async-start | bytes 3145728 | tf_op jit(solution)/shard_map/all_to_all | solution.py:90
  19.3 106.9 %all-gather.6.cloned.1.call-start = ((), (), s32[]{:S(2)}) async-start(), calls=%async_computation.1 | async-start | bytes 1310720 | tf_op jit(solution)/shard_map/all_gather | solution.py:37
  20.5 222.8 %all-reduce.3.cloned.1.call-start = ((), (), s32[]{:S(2)}) async-start(), calls=%async_computation.3 | async-start | bytes 12582912 | tf_op jit(solution)/shard_map/psum | solution.py:110
  243.4 3.6 %copy-start = (f32[1536,512]{1,0:T(8,128)S(1)}, f32[1536,512]{1,0:T(8,128)}, u32[]{:S(2)}) copy-start(f32[1536,512]{1,0:T(8,128)} %get-tuple-element.16) | copy-start | bytes 9437188
Sparse Core Ops, SparseCore 0:
  11.5 54.5 all-gather.7
  68.3 37.9 all-gather.5
  124.5 118.8 all-reduce.2
